TPU v7x, 256 devices: a whole 4x4x8 slice. The times are simulated.
256 devices in a mesh: ctx: 64 (over x, y, z_lo), tp: 4 (over z_hi, core).
Axes of the slice: x: 4, y: 4, z: 8 (z_hi: 2, z_lo: 4; z = z_hi * 4 + z_lo), core: 2. Of those that a mesh axis runs over, the one named last changes fastest.
Arguments:
- span_rows: bfloat16 [2, 2048, 3584], P(None, 'ctx'), may hold values from -6 to 6
- step_rows: bfloat16 [4, 256, 3584], P(None, 'ctx'), may hold values from -6 to 6
- lengths: int32 [2], replicated, may hold values from 4097 to 6144
- sample_prompt: int32 [256], P('ctx'), may hold values from 0 to 1
- norm_gain: float32 [3584], replicated, may hold values from 0.5 to 1.5
- query_weight: bfloat16 [3584, 3584], P('ctx', 'tp'), may hold values from -0.1875 to 0.1875
- key_weight: bfloat16 [3584, 512], P(None, 'tp'), may hold values from -0.1875 to 0.1875
- value_weight: bfloat16 [3584, 512], P(None, 'tp'), may hold values from -0.09375 to 0.09375
- query_bias: float32 [3584], P('tp'), may hold values from -16 to 16
- key_bias: float32 [512], P('tp'), may hold values from -16 to 16
- value_bias: float32 [512], P('tp'), may hold values from -3 to 3
- out_weight: bfloat16 [3584, 3584], P('tp', 'ctx'), may hold values from -0.25 to 0.25
- cache_keys: bfloat16 [2, 4096, 512], P(None, 'ctx', 'tp'), may hold values from -12 to 12
- cache_values: bfloat16 [2, 4096, 512], P(None, 'ctx', 'tp'), may hold values from -6 to 6
Outputs:
- span_out: bfloat16 [2, 2048, 3584], P(None, 'ctx', 'tp')
- dec_out: bfloat16 [4, 256, 3584], P(None, 'ctx', 'tp')
All inputs are finite; a program needn't handle non-finite values.
Results may differ from a plain program's by a relative error of at most 0.012.
The roundings to bfloat16 on the way count: a program that leaves them out, or rounds other values in their place, can miss the bound.
Values may be sent and summed in bfloat16 or wider, within the bound.
A program may use at most 128 MiB of HBM per device.

v0:
```python
import math
import jax
import jax.numpy as jnp
from jax import lax
from jax.sharding import PartitionSpec as P

HEADS = 28
KV_HEADS = 4
HEAD = 128
ROPE_BASE = 1000000.0
NORM_EPS = 1e-06
MASKED = -1e30


def turned_gather(arrays, axis, dims):
    turned = [jnp.moveaxis(a, dim, 0) for a, dim in zip(arrays, dims)]
    widths = [t[0].size for t in turned]
    both = jnp.concatenate([t.reshape(-1, w) for t, w in zip(turned, widths)], axis=1)
    filled = lax.all_gather(both, axis, axis=0, tiled=True)
    parts = jnp.split(filled, [sum(widths[:k]) for k in range(1, len(widths))], axis=1)
    return tuple(
        (
            jnp.moveaxis(b.reshape(-1, *t.shape[1:]), 0, dim)
            for b, t, dim in zip(parts, turned, dims)
        )
    )


def sent_together(arrays, axis, dim, along):
    widths = [a.shape[along] for a in arrays]
    both = jnp.concatenate(arrays, axis=along)
    filled = lax.all_gather(both, axis, axis=dim, tiled=True)
    return tuple(jnp.split(filled, [sum(widths[:k]) for k in range(1, len(widths))], axis=along))


def in_blocks(x, dim, length):
    before, after = (x.shape[:dim], x.shape[dim + 1 :])
    return jnp.moveaxis(x.reshape(*before, length, -1, *after), dim, 0)


def sum_at_owner(x, axis, dim):
    parts = in_blocks(x, dim, lax.axis_size(axis))
    arrived = lax.all_to_all(parts, axis, split_axis=0, concat_axis=0, tiled=True)
    return arrived.astype(jnp.float32).sum(axis=0)


def norm_rows(inputs, norm_gain):
    widened = inputs.astype(jnp.float32)
    inverse = lax.rsqrt(jnp.mean(widened * widened, axis=-1, keepdims=True) + NORM_EPS)
    return (widened * inverse * norm_gain).astype(jnp.bfloat16)


def rotate(vectors, positions):
    width = vectors.shape[-1]
    half = width // 2
    exponent = jnp.arange(half, dtype=jnp.float32) * (2.0 / width)
    frequency = jnp.exp(exponent * -math.log(ROPE_BASE))
    angles = positions.astype(jnp.float32)[..., None, None] * frequency
    cosine = jnp.cos(angles)
    sine = jnp.sin(angles)
    first = vectors[..., :half]
    second = vectors[..., half:]
    return jnp.concatenate(
        [first * cosine - second * sine, second * cosine + first * sine], axis=-1
    )


def project(normed, weight, bias):
    return jnp.dot(normed, weight, preferred_element_type=jnp.float32) + bias


def key_positions(count, prefix_dev, span_dev, prefix_all):
    row_index = jnp.arange(count, dtype=jnp.int32)
    device = row_index // (prefix_dev + span_dev)
    offset = row_index % (prefix_dev + span_dev)
    return jnp.where(
        offset < prefix_dev,
        device * prefix_dev + offset,
        prefix_all + device * span_dev + offset - prefix_dev,
    )


def local(
    span_rows,
    step_rows,
    lengths,
    sample_prompt,
    norm_gain,
    query_weight,
    key_weight,
    value_weight,
    query_bias,
    key_bias,
    value_bias,
    out_weight,
    cache_keys,
    cache_values,
):
    cycle_size = lax.axis_size("ctx")
    cycle_place = lax.axis_index("ctx")
    prompt_count = span_rows.shape[0]
    span_dev = span_rows.shape[1]
    prefix_dev = cache_keys.shape[1]
    kv_local = key_weight.shape[1] // HEAD
    kv_group = HEADS // KV_HEADS
    heads_local = kv_local * kv_group
    prefix_all = prefix_dev * cycle_size
    factor = HEAD ** (-0.5)
    full_query, full_out = turned_gather((query_weight, out_weight), "ctx", (0, 1))
    normed = norm_rows(span_rows, norm_gain)
    span_places = prefix_all + cycle_place * span_dev + jnp.arange(span_dev, dtype=jnp.int32)
    grid_places = jnp.broadcast_to(span_places, (prompt_count, span_dev))
    queries = rotate(
        project(normed, full_query, query_bias).reshape(prompt_count, span_dev, heads_local, HEAD),
        grid_places,
    ).astype(jnp.bfloat16)
    new_keys = rotate(
        project(normed, key_weight, key_bias).reshape(prompt_count, span_dev, kv_local, HEAD),
        grid_places,
    ).astype(jnp.bfloat16)
    new_values = project(normed, value_weight, value_bias).astype(jnp.bfloat16)
    key_block = jnp.concatenate(
        [cache_keys, new_keys.reshape(prompt_count, span_dev, kv_local * HEAD)], axis=1
    )
    value_block = jnp.concatenate([cache_values, new_values], axis=1)
    query_rows = (
        queries.reshape(prompt_count, span_dev, kv_local, kv_group, HEAD)
        .transpose(0, 2, 1, 3, 4)
        .reshape(prompt_count, kv_local, span_dev * kv_group, HEAD)
    )
    query_places = jnp.repeat(span_places, kv_group)
    row_count = span_dev * kv_group
    key_all, value_all = sent_together((key_block, value_block), "ctx", 1, 0)
    highest = jnp.full((prompt_count, kv_local, row_count), MASKED, jnp.float32)
    count = key_all.shape[1]
    places = key_positions(count, prefix_dev, span_dev, prefix_all)
    key_grid = key_all.reshape(prompt_count, count, kv_local, HEAD)
    value_grid = value_all.reshape(prompt_count, count, kv_local, HEAD)
    scores = (
        jnp.einsum("pgqd,pkgd->pgqk", query_rows, key_grid, preferred_element_type=jnp.float32)
        * factor
    )
    visible = (places[None, None, None, :] < lengths[:, None, None, None]) & (
        places[None, None, None, :] <= query_places[None, None, :, None]
    )
    scores = jnp.where(visible, scores, MASKED)
    raised = jnp.maximum(highest, jnp.max(scores, axis=-1))
    weights = jnp.where(visible, jnp.exp(scores - raised[..., None]), 0.0)
    totals = jnp.sum(weights, axis=-1)
    blended = jnp.einsum(
        "pgqk,pkgd->pgqd",
        weights.astype(jnp.bfloat16),
        value_grid,
        preferred_element_type=jnp.float32,
    )
    highest, totals, blended = (raised, totals, blended)
    span_attention = (blended / totals[..., None]).astype(jnp.bfloat16)
    span_attention = (
        span_attention.reshape(prompt_count, kv_local, span_dev, kv_group, HEAD)
        .transpose(0, 2, 1, 3, 4)
        .reshape(prompt_count, span_dev, heads_local * HEAD)
    )
    span_terms = jnp.dot(span_attention, full_out, preferred_element_type=jnp.float32)
    span_out = sum_at_owner(span_terms.astype(jnp.bfloat16), "tp", 2).astype(jnp.bfloat16)
    gathered_rows = key_all.shape[1]
    key_grid = key_all.reshape(prompt_count, gathered_rows, kv_local, HEAD)
    value_grid = value_all.reshape(prompt_count, gathered_rows, kv_local, HEAD)
    all_places = key_positions(gathered_rows, prefix_dev, span_dev, prefix_all)
    picked = sample_prompt[:, None] == jnp.arange(prompt_count, dtype=jnp.int32)[None, :]
    length_of = jnp.sum(jnp.where(picked, lengths[None, :], 0), axis=1)
    prefix_visible = picked[:, :, None] & (all_places[None, None, :] < length_of[:, None, None])
    wide_visible = prefix_visible[:, None, None, :, :]
    sample_count = step_rows.shape[1]
    step_count = step_rows.shape[0]
    step_ids = jnp.arange(step_count, dtype=jnp.int32)
    made_keys = jnp.zeros((sample_count, step_count, kv_local, HEAD), jnp.bfloat16)
    made_values = jnp.zeros((sample_count, step_count, kv_local, HEAD), jnp.bfloat16)
    outputs = []
    for step_index in range(step_count):
        normed_step = norm_rows(step_rows[step_index], norm_gain)
        places_now = length_of + step_index
        step_queries = rotate(
            project(normed_step, full_query, query_bias).reshape(sample_count, heads_local, HEAD),
            places_now,
        ).astype(jnp.bfloat16)
        step_queries = step_queries.reshape(sample_count, kv_local, kv_group, HEAD)
        fresh_keys = rotate(
            project(normed_step, key_weight, key_bias).reshape(sample_count, kv_local, HEAD),
            places_now,
        ).astype(jnp.bfloat16)
        fresh_values = (
            project(normed_step, value_weight, value_bias)
            .astype(jnp.bfloat16)
            .reshape(sample_count, kv_local, HEAD)
        )
        made_keys = made_keys.at[:, step_index].set(fresh_keys)
        made_values = made_values.at[:, step_index].set(fresh_values)
        own_visible = step_ids <= step_index
        far_scores = (
            jnp.einsum(
                "sgqd,pkgd->sgqpk", step_queries, key_grid, preferred_element_type=jnp.float32
            )
            * factor
        )
        far_scores = jnp.where(wide_visible, far_scores, MASKED)
        near_scores = (
            jnp.einsum(
                "sgqd,stgd->sgqt", step_queries, made_keys, preferred_element_type=jnp.float32
            )
            * factor
        )
        near_scores = jnp.where(own_visible, near_scores, MASKED)
        highest_now = jnp.maximum(jnp.max(far_scores, axis=(3, 4)), jnp.max(near_scores, axis=-1))
        far_weights = jnp.where(
            wide_visible, jnp.exp(far_scores - highest_now[..., None, None]), 0.0
        )
        near_weights = jnp.where(own_visible, jnp.exp(near_scores - highest_now[..., None]), 0.0)
        totals_now = jnp.sum(far_weights, axis=(3, 4)) + jnp.sum(near_weights, axis=-1)
        blended_now = jnp.einsum(
            "sgqpk,pkgd->sgqd",
            far_weights.astype(jnp.bfloat16),
            value_grid,
            preferred_element_type=jnp.float32,
        )
        blended_now = blended_now + jnp.einsum(
            "sgqt,stgd->sgqd",
            near_weights.astype(jnp.bfloat16),
            made_values,
            preferred_element_type=jnp.float32,
        )
        step_attention = (
            (blended_now / totals_now[..., None])
            .astype(jnp.bfloat16)
            .reshape(sample_count, heads_local * HEAD)
        )
        outputs.append(step_attention)
    stacked = jnp.stack(outputs)
    decode_terms = jnp.dot(stacked, full_out, preferred_element_type=jnp.float32)
    dec_out = sum_at_owner(decode_terms.astype(jnp.bfloat16), "tp", 2).astype(jnp.bfloat16)
    return (span_out, dec_out)


def solution(mesh):
    return jax.shard_map(
        local,
        mesh=mesh,
        in_specs=(
            P(None, "ctx", None),
            P(None, "ctx", None),
            P(),
            P("ctx"),
            P(),
            P("ctx", "tp"),
            P(None, "tp"),
            P(None, "tp"),
            P("tp"),
            P("tp"),
            P("tp"),
            P("tp", "ctx"),
            P(None, "ctx", "tp"),
            P(None, "ctx", "tp"),
        ),
        out_specs=(P(None, "ctx", "tp"), P(None, "ctx", "tp")),
        check_vma=False,
    )
```

profile of v0, /device:TPU:1, one launch (start us, length us, event | category | flops | bytes accessed | tf_op | source)
XLA Modules:
  0.0 852.5 jit_solution(219215414746392253)
XLA Ops:
  7.3 1.8 pad_maximum_fusion
  9.2 1.2 fusion.129
  10.4 1.7 fusion.62
  12.1 0.1 fusion.200
  12.2 1.4 fusion.63
  13.6 0.7 maximum_maximum_fusion
  14.4 0.1 le.41
  14.6 0.2 fusion.166
  14.9 0.3 fusion.118
  15.3 0.3 fusion.107
  15.5 0.1 fusion.274
  15.8 0.3 fusion.104
  16.1 0.3 fusion.105
  16.4 0.3 fusion.106
  16.7 0.1 fusion.258
  16.8 0.1 multiply_cosine_fusion.5
  17.0 0.1 multiply_cosine_fusion.1
  17.3 0.1 broadcast_and_fusion
  17.4 2.0 broadcast_compare_fusion
  19.4 345.0 %all-gather.3.cloned.1.call-done = bf16[3584,1792]{1,0:T(8,128)(2,1)} async-done(((bf16[56,1792]{1,0:T(8,128)(2,1)}), bf16[3584,1792]{1,0:T(8,128)(2,1)}) %all-gather.3.cloned.1.call-update) | async-done | bytes 12845072 | tf_op jit(solution)/shard_map/all_gather | solution.py:19
  364.5 3.8 fusion.91
  368.3 3.8 fusion.88
  372.1 3.8 fusion.94
  376.0 3.8 fusion.97
  379.9 0.2 fusion.311
  380.1 350.8 %all-gather.5.cloned.1.call-done = bf16[4,6144,128]{2,1,0:T(8,128)(2,1)} async-done(((bf16[4,96,128]{2,1,0:T(8,128)(2,1)}), bf16[4,6144,128]{2,1,0:T(8,128)(2,1)}) %all-gather.5.cloned.1.call-update) | async-done | bytes 6291472 | tf_op jit(solution)/shard_map/all_gather | solution.py:32
  730.9 3.3 fusion.310
  734.3 0.2 fusion.313
  734.5 0.1 copy-done.16
  734.6 1.3 fusion.312
  736.0 0.2 fusion.315
  736.3 1.3 fusion.314
  737.7 0.8 fusion.309
  738.5 1.3 fusion.308
  740.0 1.8 fusion.51
  741.8 0.6 fusion.64
  742.4 0.2 fusion.87
  742.6 0.3 fusion.117
  743.0 0.8 fusion.67
  743.9 0.2 fusion.86
  744.1 0.3 fusion.115
  744.4 0.6 fusion.70
  745.1 0.2 fusion.85
  745.3 0.3 fusion.113
  745.7 4.1 fusion.59
  749.8 0.2 subtract_convert_fusion
  750.0 0.1 copy.45
  750.2 0.1 copy.44
  750.3 4.8 fusion.307
  755.2 3.0 fusion
  758.2 5.2 fusion.124
  763.4 0.1 reshape_transpose_reshape.4
  763.7 3.0 fusion.73
  766.7 0.2 fusion.84
  767.0 4.7 fusion.19
  771.6 0.7 copy.96
  772.3 47.0 %all-to-all-start.1 = ((bf16[4,4,4,896]{3,2,1,0:T(4,128)(2,1)}), bf16[4,4,4,896]{3,2,1,0:T(4,128)(2,1)S(1)}, u32[]{:S(2)}, u32[]{:S(2)}) async-start(bf16[4,4,4,896]{3,2,1,0:T(4,128)(2,1)} %bitcast.277), calls=%async_computation.1 | async-start | bytes 229376 | tf_op jit(solution)/shard_map/all_to_all | solution.py:43
  819.3 4.9 fusion.18
  824.2 0.8 copy.95
  825.1 1.6 all-to-all-done.1
  826.7 5.6 all-to-all-start
  832.3 0.7 reduce_sum.175
  832.9 12.0 %all-to-all-done = bf16[4,2,32,896]{3,2,1,0:T(8,128)(2,1)S(1)} async-done(((bf16[4,2,32,896]{3,2,1,0:T(8,128)(2,1)}), bf16[4,2,32,896]{3,2,1,0:T(8,128)(2,1)S(1)}, u32[]{:S(2)}, u32[]{:S(2)}) %all-to-all-start) | async-done | bytes 458784 | tf_op jit(solution)/shard_map/all_to_all | solution.py:43
  844.9 0.7 reduce_sum.161
  (88 shorter events, 1.9 us)
Async XLA Ops:
  7.2 5.1 copy-start
  7.2 7.6 copy-start.3
  7.2 8.1 copy-start.1
  7.2 8.1 copy-start.10
  7.2 7.6 copy-start.11
  7.2 6.4 copy-start.8
  7.2 6.4 copy-start.9
  7.3 7.4 copy-start.4
  7.3 7.9 copy-start.13
  7.3 7.9 copy-start.17
  7.3 357.2 %all-gather.3.cloned.1.call-start = ((), (), s32[]{:S(2)}) async-start(), calls=%async_computation.2 | async-start | bytes 13045760 | tf_op jit(solution)/shard_map/all_gather | solution.py:19
  9.1 721.8 %all-gather.5.cloned.1.call-start = ((), (), s32[]{:S(2)}) async-start(), calls=%async_computation.3 | async-start | bytes 6389760 | tf_op jit(solution)/shard_map/all_gather | solution.py:32
  14.6 723.1 %copy-start.14 = (pred[4]{0:T(512)(128)(4,1)}, pred[4]{0:T(512)(128)(4,1)S(1)}, u32[]{:S(2)}) copy-start(pred[4]{0:T(512)(128)(4,1)S(1)} %iota_compare_fusion.2) | copy-start | bytes 16
  14.8 349.6 %copy-start.7 = (f32[896]{0:T(1024)S(1)}, f32[896]{0:T(1024)}, u32[]{:S(2)}) copy-start(f32[896]{0:T(1024)} %param.38) | copy-start | bytes 10756
  730.9 3.7 copy-start.16
  739.8 2.0 copy-start.5
  744.4 1.3 copy-start.6
  750.3 4.9 copy-start.2
  758.2 5.4 copy-start.12
  758.2 5.4 copy-start.15
  772.3 54.4 %all-to-all-start.1 = ((bf16[4,4,4,896]{3,2,1,0:T(4,128)(2,1)}), bf16[4,4,4,896]{3,2,1,0:T(4,128)(2,1)S(1)}, u32[]{:S(2)}, u32[]{:S(2)}) async-start(bf16[4,4,4,896]{3,2,1,0:T(4,128)(2,1)} %bitcast.277), calls=%async_computation.1 | async-start | bytes 229376 | tf_op jit(solution)/shard_map/all_to_all | solution.py:43
  826.7 18.3 %all-to-all-start = ((bf16[4,2,32,896]{3,2,1,0:T(8,128)(2,1)}), bf16[4,2,32,896]{3,2,1,0:T(8,128)(2,1)S(1)}, u32[]{:S(2)}, u32[]{:S(2)}) async-start(bf16[4,2,32,896]{3,2,1,0:T(8,128)(2,1)} %bitcast.275), calls=%async_computation | async-start | bytes 917504 | tf_op jit(solution)/shard_map/all_to_all | solution.py:43
Sparse Core Ops, SparseCore 0:
  9.9 354.5 all-gather.2
  366.8 363.9 all-gather.4
where the time goes:
time: 853 us; the launch traced here: 852 us
  waiting for transfers between devices  709 us (83%)
  matrix products  58.9 us (7%)
  starting transfers between devices  52.7 us (6%)
  between operations  14.6 us (2%)
  other arithmetic  14.3 us (2%)
    all_gather x1, waiting for transfers between devices, sent_together(): filled = lax.all_gather(both, axis, axis=dim, tiled=True)  351 us
    all_gather x1, waiting for transfers between devices, turned_gather(): filled = lax.all_gather(both, axis, axis=0, tiled=True)  345 us
    all_to_all x2, starting transfers between devices, sum_at_owner(): lax.all_to_all(parts, axis, split_axis=0, concat_axis=0, tiled=True)  52.6 us
    dot_general x15, matrix products, project(): return jnp.dot(normed, weight, preferred_element_type=jnp.float32) + bias  24.7 us
  transfers between devices with their start and end apart: 4, of which 4 were waited for; matrix products, arithmetic and copies ran while one was open for 4% of the time, Pallas kernels for 0%

commit v1 on v0

--- a/solution.py
+++ b/solution.py
@@ -16,7 +16,12 @@
     turned = [jnp.moveaxis(a, dim, 0) for a, dim in zip(arrays, dims)]
     widths = [t[0].size for t in turned]
     both = jnp.concatenate([t.reshape(-1, w) for t, w in zip(turned, widths)], axis=1)
-    filled = lax.all_gather(both, axis, axis=0, tiled=True)
+    filled = jnp.concatenate(
+        jax.lax.all_to_all(
+            jnp.stack(jax.lax.psum(1, axis) * [both], axis=0), axis, split_axis=0, concat_axis=0
+        ),
+        0,
+    )
     parts = jnp.split(filled, [sum(widths[:k]) for k in range(1, len(widths))], axis=1)
     return tuple(
         (

time: 853 us -> 570 us (0.67)
  waiting for transfers between devices: 709 us -> 420 us
    all_to_all x0 -> x1, waiting for transfers between devices: none -> 385 us  [turned_gather(): jax.lax.all_to_all(jnp.stack(jax.lax.psum(1, axis) * [both], axis=0), axi...]
    all_gather x1 -> x0, waiting for transfers between devices: 345 us -> none  [turned_gather(): filled = lax.all_gather(both, axis, axis=0, tiled=True)]
    all_gather x1, waiting for transfers between devices: 351 us -> 24.5 us  [sent_together(): filled = lax.all_gather(both, axis, axis=dim, tiled=True)]
    all_to_all x0 -> x1, starting transfers between devices: none -> 12.9 us  [turned_gather(): jax.lax.all_to_all(jnp.stack(jax.lax.psum(1, axis) * [both], axis=0), axi...]
    all_to_all x2, starting transfers between devices: 52.6 us -> 43.7 us  [sum_at_owner(): lax.all_to_all(parts, axis, split_axis=0, concat_axis=0, tiled=True)]
  transfers between devices with their start and end apart: 4 -> 4, of which waited for: 4 -> 3; matrix products, arithmetic and copies ran while one was open for 4% -> 8% of each run, Pallas kernels for 0% -> 0%
where the time goes in v1:
time: 570 us; the launch traced here: 569 us
  waiting for transfers between devices  420 us (74%)
  starting transfers between devices  56.6 us (10%)
  matrix products  55.4 us (10%)
  between operations  14.7 us (3%)
  other arithmetic  13.8 us (2%)
  local copies, waits for them, and re-layouts  8.98 us (2%)
    all_to_all x1, waiting for transfers between devices, turned_gather(): jax.lax.all_to_all(jnp.stack(jax.lax.psum(1, axis) * [both], axis=0), axi...  385 us
    all_to_all x2, starting transfers between devices, sum_at_owner(): lax.all_to_all(parts, axis, split_axis=0, concat_axis=0, tiled=True)  43.7 us
    all_gather x1, waiting for transfers between devices, sent_together(): filled = lax.all_gather(both, axis, axis=dim, tiled=True)  24.5 us
    dot_general x15, matrix products, project(): return jnp.dot(normed, weight, preferred_element_type=jnp.float32) + bias  22.4 us
    all_to_all x1, starting transfers between devices, turned_gather(): jax.lax.all_to_all(jnp.stack(jax.lax.psum(1, axis) * [both], axis=0), axi...  12.9 us
  transfers between devices with their start and end apart: 4, of which 3 were waited for; matrix products, arithmetic and copies ran while one was open for 8% of the time, Pallas kernels for 0%

profile of v1, /device:TPU:1, one launch (start us, length us, event | category | flops | bytes accessed | tf_op | source)
XLA Modules:
  0.0 569.3 jit_solution(8174812874599158945)
XLA Ops:
  7.2 1.0 pad_maximum_fusion
  8.2 5.4 stack.4
  13.7 12.9 %all-to-all-start = ((bf16[64,56,1792]{2,1,0:T(8,128)(2,1)}), bf16[64,56,1792]{2,1,0:T(8,128)(2,1)}, u32[]{:S(2)}, u32[]{:S(2)}) async-start(bf16[64,56,1792]{2,1,0:T(8,128)(2,1)} %stack.4), calls=%async_computation | async-start | bytes 25690112 | tf_op jit(solution)/shard_map/all_to_all | solution.py:20
  26.7 0.2 fusion.129
  27.0 0.3 fusion.62
  27.3 0.1 fusion.200
  27.5 0.3 fusion.63
  27.8 0.7 maximum_maximum_fusion
  28.6 0.2 fusion.166
  29.1 0.3 fusion.118
  29.3 0.6 pad_bitcast_fusion
  30.0 0.3 fusion.107
  30.6 0.3 fusion.104
  30.9 0.3 fusion.105
  31.2 0.3 fusion.106
  31.5 0.1 fusion.258
  31.6 0.1 multiply_cosine_fusion.5
  31.8 0.8 multiply_cosine_fusion.1
  32.6 0.7 broadcast_compare_fusion.2
  33.5 2.0 broadcast_compare_fusion
  35.4 384.9 %all-to-all-done = bf16[64,56,1792]{2,1,0:T(8,128)(2,1)} async-done(((bf16[64,56,1792]{2,1,0:T(8,128)(2,1)}), bf16[64,56,1792]{2,1,0:T(8,128)(2,1)}, u32[]{:S(2)}, u32[]{:S(2)}) %all-to-all-start) | async-done | bytes 12845088 | tf_op jit(solution)/shard_map/all_to_all | solution.py:20
  420.3 3.8 fusion.88
  424.2 3.8 fusion.91
  428.0 3.8 fusion.94
  431.9 3.8 fusion.97
  435.8 0.2 fusion.311
  436.1 0.2 fusion.313
  436.5 0.2 fusion.315
  436.8 0.2 fusion.309
  437.0 24.5 %all-gather.2.cloned.1.call-done = bf16[4,6144,128]{2,1,0:T(8,128)(2,1)} async-done(((bf16[4,96,128]{2,1,0:T(8,128)(2,1)}), bf16[4,6144,128]{2,1,0:T(8,128)(2,1)}) %all-gather.2.cloned.1.call-update) | async-done | bytes 6291472 | tf_op jit(solution)/shard_map/all_gather | solution.py:37
  461.6 3.3 fusion.308
  464.9 0.4 copy-done.29
  465.3 1.3 fusion.314
  466.6 1.3 fusion.312
  467.9 1.3 fusion.310
  469.5 1.8 fusion.51
  471.3 0.6 fusion.64
  472.0 0.2 fusion.87
  472.2 0.4 fusion.117
  472.6 0.6 fusion.67
  473.2 0.2 fusion.86
  473.5 0.3 fusion.115
  473.8 0.6 fusion.70
  474.5 0.2 fusion.85
  474.7 0.3 fusion.113
  475.1 4.1 fusion.59
  479.3 2.5 fusion.73
  481.8 0.2 fusion.84
  482.1 4.7 fusion.19
  486.8 0.7 copy.96
  487.5 36.5 %all-to-all-start.2 = ((bf16[4,4,4,896]{3,2,1,0:T(4,128)(2,1)}), bf16[4,4,4,896]{3,2,1,0:T(4,128)(2,1)S(1)}, u32[]{:S(2)}, u32[]{:S(2)}) async-start(bf16[4,4,4,896]{3,2,1,0:T(4,128)(2,1)} %bitcast.278), calls=%async_computation.2 | async-start | bytes 229376 | tf_op jit(solution)/shard_map/all_to_all | solution.py:48
  524.1 0.2 subtract_convert_fusion
  524.2 0.1 copy.44
  524.4 0.1 copy.45
  524.6 4.8 fusion.307
  529.4 3.0 fusion
  532.4 5.2 fusion.124
  537.7 0.1 reshape_transpose_reshape.4
  537.8 4.9 fusion.18
  542.7 0.8 copy.95
  543.5 7.2 %all-to-all-start.1 = ((bf16[4,2,32,896]{3,2,1,0:T(8,128)(2,1)}), bf16[4,2,32,896]{3,2,1,0:T(8,128)(2,1)S(1)}, u32[]{:S(2)}, u32[]{:S(2)}) async-start(bf16[4,2,32,896]{3,2,1,0:T(8,128)(2,1)} %bitcast.276), calls=%async_computation.1 | async-start | bytes 917504 | tf_op jit(solution)/shard_map/all_to_all | solution.py:48
  550.7 0.7 reduce_sum.175
  551.4 10.4 %all-to-all-done.1 = bf16[4,2,32,896]{3,2,1,0:T(8,128)(2,1)S(1)} async-done(((bf16[4,2,32,896]{3,2,1,0:T(8,128)(2,1)}), bf16[4,2,32,896]{3,2,1,0:T(8,128)(2,1)S(1)}, u32[]{:S(2)}, u32[]{:S(2)}) %all-to-all-start.1) | async-done | bytes 458784 | tf_op jit(solution)/shard_map/all_to_all | solution.py:48
  561.8 0.7 reduce_sum.161
  (114 shorter events, 2.2 us)
Async XLA Ops:
  7.2 20.3 %copy-start = (bf16[3584,128]{1,0:T(8,128)(2,1)S(1)}, bf16[3584,128]{1,0:T(8,128)(2,1)}, u32[]{:S(2)}) copy-start(bf16[3584,128]{1,0:T(8,128)(2,1)} %param.37) | copy-start | bytes 2752516
  13.6 13.1 %copy-start.5 = (bf16[2,32,3584]{2,1,0:T(8,128)(2,1)S(1)}, bf16[2,32,3584]{2,1,0:T(8,128)(2,1)}, u32[]{:S(2)}) copy-start(bf16[2,32,3584]{2,1,0:T(8,128)(2,1)} %param.30) | copy-start | bytes 1376260
  13.7 13.3 %copy-start.1 = (bf16[3584,128]{1,0:T(8,128)(2,1)S(1)}, bf16[3584,128]{1,0:T(8,128)(2,1)}, u32[]{:S(2)}) copy-start(bf16[3584,128]{1,0:T(8,128)(2,1)} %param.36) | copy-start | bytes 2752516
  13.7 13.3 %copy-start.3 = (f32[3584]{0:T(1024)S(1)}, f32[3584]{0:T(1024)}, u32[]{:S(2)}) copy-start(f32[3584]{0:T(1024)} %param.34) | copy-start | bytes 43012
  13.7 13.3 %copy-start.13 = (f32[128]{0:T(128)S(1)}, f32[128]{0:T(128)}, u32[]{:S(2)}) copy-start(f32[128]{0:T(128)} %param.39) | copy-start | bytes 1540
  13.7 13.8 %copy-start.14 = (f32[128]{0:T(128)S(1)}, f32[128]{0:T(128)}, u32[]{:S(2)}) copy-start(f32[128]{0:T(128)} %param.40) | copy-start | bytes 1540
  13.7 406.6 %all-to-all-start = ((bf16[64,56,1792]{2,1,0:T(8,128)(2,1)}), bf16[64,56,1792]{2,1,0:T(8,128)(2,1)}, u32[]{:S(2)}, u32[]{:S(2)}) async-start(bf16[64,56,1792]{2,1,0:T(8,128)(2,1)} %stack.4), calls=%async_computation | async-start | bytes 25690112 | tf_op jit(solution)/shard_map/all_to_all | solution.py:20
  26.6 1.2 copy-start.11
  26.6 1.2 copy-start.12
  26.6 2.0 copy-start.4
  26.6 3.3 copy-start.20
  26.6 3.3 copy-start.30
  26.7 434.9 %all-gather.2.cloned.1.call-start = ((), (), s32[]{:S(2)}) async-start(), calls=%async_computation.3 | async-start | bytes 6389760 | tf_op jit(solution)/shard_map/all_gather | solution.py:37
  27.0 3.9 copy-start.18
  28.6 407.2 %copy-start.27 = (pred[4]{0:T(512)(128)(4,1)}, pred[4]{0:T(512)(128)(4,1)S(1)}, u32[]{:S(2)}) copy-start(pred[4]{0:T(512)(128)(4,1)S(1)} %iota_compare_fusion.5) | copy-start | bytes 16
  28.6 407.5 %copy-start.25 = (pred[4]{0:T(512)(128)(4,1)}, pred[4]{0:T(512)(128)(4,1)S(1)}, u32[]{:S(2)}) copy-start(pred[4]{0:T(512)(128)(4,1)S(1)} %iota_compare_fusion.4) | copy-start | bytes 16
  28.6 407.8 %copy-start.23 = (pred[4]{0:T(512)(128)(4,1)}, pred[4]{0:T(512)(128)(4,1)S(1)}, u32[]{:S(2)}) copy-start(pred[4]{0:T(512)(128)(4,1)S(1)} %iota_compare_fusion.3) | copy-start | bytes 16
  28.9 408.0 %copy-start.21 = (pred[4]{0:T(512)(128)(4,1)}, pred[4]{0:T(512)(128)(4,1)S(1)}, u32[]{:S(2)}) copy-start(pred[4]{0:T(512)(128)(4,1)S(1)} %iota_compare_fusion.2) | copy-start | bytes 16
  29.1 391.3 %copy-start.10 = (f32[896]{0:T(1024)S(1)}, f32[896]{0:T(1024)}, u32[]{:S(2)}) copy-start(f32[896]{0:T(1024)} %param.38) | copy-start | bytes 10756
  31.2 393.0 %copy-start.15 = (f32[4]{0:T(128)}, f32[4]{0:T(128)S(1)}, u32[]{:S(2)}) copy-start(f32[4]{0:T(128)S(1)} %add_rsqrt_fusion.3) | copy-start | bytes 52
  461.6 3.7 copy-start.29
  467.9 1.3 copy-start.24
  467.9 1.4 copy-start.26
  467.9 1.5 copy-start.28
  471.3 0.7 copy-start.17
  471.3 0.9 copy-start.16
  473.8 1.3 copy-start.6
  473.8 1.3 copy-start.19
  475.1 4.1 copy-start.22
  482.1 41.9 %copy-start.7 = (f32[2,32,64]{2,1,0:T(8,128)S(1)}, f32[2,32,64]{2,1,0:T(8,128)}, u32[]{:S(2)}) copy-start(f32[2,32,64]{2,1,0:T(8,128)} %get-tuple-element.134) | copy-start | bytes 49156
  482.1 41.9 %copy-start.8 = (f32[2,32,64]{2,1,0:T(8,128)S(1)}, f32[2,32,64]{2,1,0:T(8,128)}, u32[]{:S(2)}) copy-start(f32[2,32,64]{2,1,0:T(8,128)} %get-tuple-element.135) | copy-start | bytes 49156
  482.1 42.4 %copy-start.9 = (pred[2,6144]{1,0:T(4,128)(4,1)S(1)}, pred[2,6144]{1,0:T(4,128)(4,1)}, u32[]{:S(2)}) copy-start(pred[2,6144]{1,0:T(4,128)(4,1)} %broadcast_compare_fusion.2) | copy-start | bytes 36868
  487.5 56.0 %all-to-all-start.2 = ((bf16[4,4,4,896]{3,2,1,0:T(4,128)(2,1)}), bf16[4,4,4,896]{3,2,1,0:T(4,128)(2,1)S(1)}, u32[]{:S(2)}, u32[]{:S(2)}) async-start(bf16[4,4,4,896]{3,2,1,0:T(4,128)(2,1)} %bitcast.278), calls=%async_computation.2 | async-start | bytes 229376 | tf_op jit(solution)/shard_map/all_to_all | solution.py:48
  524.6 4.9 copy-start.2
  543.5 18.2 %all-to-all-start.1 = ((bf16[4,2,32,896]{3,2,1,0:T(8,128)(2,1)}), bf16[4,2,32,896]{3,2,1,0:T(8,128)(2,1)S(1)}, u32[]{:S(2)}, u32[]{:S(2)}) async-start(bf16[4,2,32,896]{3,2,1,0:T(8,128)(2,1)} %bitcast.276), calls=%async_computation.1 | async-start | bytes 917504 | tf_op jit(solution)/shard_map/all_to_all | solution.py:48
Sparse Core Ops, SparseCore 0:
  29.8 431.7 all-gather.1
